TPU v7x, 128 devices: a whole 4x4x4 slice. The times are simulated.
128 devices in a mesh: attn: 8 (over x, core), ffn: 16 (over y, z).
Axes of the slice: x: 4, y: 4, z: 4, core: 2. Of those that a mesh axis runs over, the one named last changes fastest.
Arguments:
- queries: bfloat16 [1024, 2, 64, 576], P(('attn', 'ffn')), may hold values from -9 to 9
- latent_cache: bfloat16 [1024, 512, 576], P(('attn', 'ffn')), may hold values from -4 to 4
- fresh_latent: bfloat16 [1024, 2, 576], P(('attn', 'ffn')), may hold values from -4 to 4
- lengths: int32 [1024], P(('attn', 'ffn')), may hold values from 1 to 512, 262144 in all
- handoff: int32 [16, 8], P('ffn'), may hold values 0 or 1
- residual: bfloat16 [1024, 2, 7168], P(('attn', 'ffn')), may hold values from -30 to 30
- value_up_matrix: bfloat16 [64, 512, 128], P('ffn'), may hold values from -0.5 to 0.5
- output_weight: bfloat16 [8192, 7168], P('ffn'), may hold values from -0.1875 to 0.1875
- norm_gain: float32 [7168], replicated, may hold values from 0.3 to 3
- router: bfloat16 [7168, 16], replicated, may hold values from -0.0625 to 0.0625
- expert_ids: int32 [1024, 2, 2], P('attn'), may hold values from 0 to 15, all different within a row; in each aligned block of 256 rows (0 to 255, 256 to 511, ..., all dimensions but the last counted through in order) at most 64 rows name the same one
- gate_weight: bfloat16 [16, 7168, 2048], P('ffn', None, 'attn'), may hold values from -0.0625 to 0.0625
- up_weight: bfloat16 [16, 7168, 2048], P('ffn', None, 'attn'), may hold values from -0.0625 to 0.0625
- down_weight: bfloat16 [16, 2048, 7168], P('ffn', 'attn'), may hold values from -0.125 to 0.125
Outputs:
- attended: bfloat16 [1024, 2, 7168], P(('attn', 'ffn'))
- expert_out: bfloat16 [1024, 2, 7168], P(('attn', 'ffn'))
Inputs may be any that keep to these rules, and one draw needn't show every extreme that they name: `expert_ids`: the 2 ids of a token differ. In each aligned block of 256 tokens (the requests of one index of attn, all new tokens of each, in order) no expert is chosen by more than 64 tokens, and some expert is chosen by exactly 64 in some block.
All inputs are finite; a program needn't handle non-finite values. No bound on the sum of `lengths` or of `handoff` on one device may be relied on, other than what follows from the above.
Results may differ from a plain program's by a relative error of at most 0.014.
Values may be sent and summed in bfloat16 or wider, within the bound.
A program may use at most 128 MiB of HBM per device.

v0:
```python
import jax
import jax.numpy as jnp
from jax import lax
from jax.sharding import PartitionSpec as P

KV_RANK = 512
score_scale = 192.0 ** (-0.5)
norm_epsilon = 1e-06


def shifted(value, axis, by):
    count = lax.axis_size(axis)
    return lax.ppermute(value, axis, [(i, (i + by) % count) for i in range(count)])


def attend_block(queries, latent_cache, fresh_latent, lengths):
    req_count, steps_here, heads_here, latent_width = queries.shape
    cache_span = latent_cache.shape[1]
    row_count = steps_here * heads_here
    rows_flat = queries.reshape(req_count, row_count, latent_width)
    old_scores = (
        jnp.einsum("rqc,rnc->rqn", rows_flat, latent_cache, preferred_element_type=jnp.float32)
        * score_scale
    )
    position = lax.broadcasted_iota(jnp.int32, (1, 1, cache_span), 2)
    old_scores = jnp.where(position < lengths[:, None, None], old_scores, -jnp.inf)
    new_scores = (
        jnp.einsum("rqc,rjc->rqj", rows_flat, fresh_latent, preferred_element_type=jnp.float32)
        * score_scale
    )
    row_step = lax.broadcasted_iota(jnp.int32, (1, row_count, steps_here), 1) // heads_here
    column_step = lax.broadcasted_iota(jnp.int32, (1, row_count, steps_here), 2)
    new_scores = jnp.where(column_step <= row_step, new_scores, -jnp.inf)
    row_peak = jnp.maximum(jnp.max(old_scores, axis=2), jnp.max(new_scores, axis=2))[:, :, None]
    old_exp = jnp.exp(old_scores - row_peak)
    new_exp = jnp.exp(new_scores - row_peak)
    denominator = jnp.sum(old_exp, axis=2, keepdims=True) + jnp.sum(new_exp, axis=2, keepdims=True)
    old_probs = (old_exp / denominator).astype(jnp.bfloat16)
    new_probs = (new_exp / denominator).astype(jnp.bfloat16)
    latent_mix = jnp.einsum(
        "rqn,rnc->rqc", old_probs, latent_cache[:, :, :KV_RANK], preferred_element_type=jnp.float32
    )
    latent_mix = latent_mix + jnp.einsum(
        "rqj,rjc->rqc", new_probs, fresh_latent[:, :, :KV_RANK], preferred_element_type=jnp.float32
    )
    return latent_mix.astype(jnp.bfloat16).reshape(req_count, steps_here, heads_here, KV_RANK)


def rms_normalize(state, norm_gain):
    scale_rows = lax.rsqrt(jnp.mean(state * state, axis=-1, keepdims=True) + norm_epsilon)
    return (state * scale_rows * norm_gain).astype(jnp.bfloat16)


def local(
    queries,
    latent_cache,
    fresh_latent,
    lengths,
    handoff,
    residual,
    value_up_matrix,
    output_weight,
    norm_gain,
    router,
    expert_ids,
    gate_weight,
    up_weight,
    down_weight,
):
    moved_flag = handoff[0] == 1
    moved_here = moved_flag[:, None, None, None]
    arrived = shifted((queries, latent_cache, fresh_latent, lengths), "attn", 1)
    queries_now = jnp.where(moved_here, arrived[0], queries)
    cache_now = jnp.where(moved_here[:, :, :, 0], arrived[1], latent_cache)
    fresh_now = jnp.where(moved_here[:, :, :, 0], arrived[2], fresh_latent)
    lengths_now = jnp.where(moved_flag, arrived[3], lengths)
    latent_out = attend_block(queries_now, cache_now, fresh_now, lengths_now)
    heads_local = value_up_matrix.shape[0]
    model_width = output_weight.shape[1]
    head_weight = output_weight.reshape(heads_local, value_up_matrix.shape[2], model_width)
    value_rows = jnp.einsum(
        "olfb,fbw->olfw",
        lax.all_to_all(latent_out, "ffn", split_axis=2, concat_axis=0, tiled=True),
        value_up_matrix,
        preferred_element_type=jnp.float32,
    ).astype(jnp.bfloat16)
    partial_out = jnp.einsum(
        "rshv,hvd->rsd", value_rows, head_weight, preferred_element_type=jnp.float32
    )
    req_dev = residual.shape[0]
    steps_here = residual.shape[1]
    ffn_index = lax.axis_index("ffn")
    local_token_rows = residual.astype(jnp.float32)
    placed_rows = lax.dynamic_update_slice(
        jnp.zeros_like(partial_out), local_token_rows, (ffn_index * req_dev, 0, 0)
    )
    state_rows = lax.psum(partial_out + placed_rows, "ffn")
    own_state = lax.dynamic_slice_in_dim(state_rows, ffn_index * req_dev, req_dev, 0)
    normed_rows = rms_normalize(state_rows, norm_gain)
    attended = own_state.astype(jnp.bfloat16)
    row_req = normed_rows.shape[0]
    row_tokens = row_req * steps_here
    normed_flat = normed_rows.reshape(row_tokens, model_width)
    expert_count = router.shape[1]
    logits = jnp.dot(normed_flat, router, preferred_element_type=jnp.float32)
    affinity = jax.nn.sigmoid(logits)
    ids_flat = expert_ids.reshape(row_tokens, expert_ids.shape[2])
    onehot = ids_flat[:, :, None] == lax.broadcasted_iota(jnp.int32, (1, 1, expert_count), 2)
    chosen = jnp.sum(jnp.where(onehot, affinity[:, None, :], 0.0), axis=2)
    gate_fraction_value = 2.5 * chosen / jnp.sum(chosen, axis=1, keepdims=True)
    routed_here = ids_flat == ffn_index
    token_weight = jnp.sum(jnp.where(routed_here, gate_fraction_value, 0.0), axis=1)
    token_hit = jnp.sum(routed_here.astype(jnp.int32), axis=1)
    slot_rank = jnp.cumsum(token_hit) - 1
    capacity = 4 * steps_here * req_dev
    slot_ids = lax.broadcasted_iota(jnp.int32, (capacity, row_tokens), 0)
    selector = ((token_hit[None, :] == 1) & (slot_rank[None, :] == slot_ids)).astype(jnp.bfloat16)
    expert_input = jnp.dot(selector, normed_flat, preferred_element_type=jnp.float32).astype(
        jnp.bfloat16
    )
    gate_local = gate_weight[0]
    up_local = up_weight[0]
    down_local = down_weight[0]
    rows_in = lax.all_gather(expert_input, "attn", axis=0, tiled=True)
    gate_part = jnp.dot(rows_in, gate_local, preferred_element_type=jnp.float32)
    up_part = jnp.dot(rows_in, up_local, preferred_element_type=jnp.float32)
    hidden_all = (jax.nn.silu(gate_part) * up_part).astype(jnp.bfloat16)
    rows_in = hidden_all
    expert_rows = lax.psum_scatter(
        jnp.dot(rows_in, down_local, preferred_element_type=jnp.float32),
        "attn",
        scatter_dimension=0,
        tiled=True,
    ).astype(jnp.bfloat16)
    returned = (
        jnp.einsum("ct,cd->td", selector, expert_rows, preferred_element_type=jnp.float32)
        * token_weight[:, None]
    )
    summed = lax.psum_scatter(
        returned.reshape(row_req, steps_here, model_width), "ffn", scatter_dimension=0, tiled=True
    )
    return (attended, summed.astype(jnp.bfloat16))


def solution(mesh):
    return jax.shard_map(
        local,
        mesh=mesh,
        in_specs=(
            P(("attn", "ffn"), None, None, None),
            P(("attn", "ffn"), None, None),
            P(("attn", "ffn"), None, None),
            P(("attn", "ffn")),
            P("ffn", None),
            P(("attn", "ffn"), None, None),
            P("ffn", None, None),
            P("ffn", None),
            P(),
            P(),
            P("attn", None, None),
            P("ffn", None, "attn"),
            P("ffn", None, "attn"),
            P("ffn", "attn", None),
        ),
        out_specs=(P(("attn", "ffn"), None, None), P(("attn", "ffn"), None, None)),
        check_vma=False,
    )
```

profile of v0, /device:TPU:0, one launch (start us, length us, event | category | flops | bytes accessed | tf_op | source)
XLA Modules:
  0.0 625.4 jit_solution(17319362532799770855)
XLA Ops:
  7.2 0.0 collective-permute-start.2
  7.2 1.7 collective-permute-start.3
  8.9 0.0 collective-permute-start.1
  9.0 1.6 collective-permute-start
  10.5 7.7 %copy.103 = bf16[8,512,576]{2,1,0:T(8,128)(2,1)} copy(bf16[8,512,576]{1,2,0:T(8,128)(2,1)} %param.15) | data formatting | bytes 9437184 | tf_op args[1]
  18.3 58.3 %collective-permute-done = s32[8]{0:T(128)S(1)} collective-permute-done((s32[8]{0:T(128)}, s32[8]{0:T(128)S(1)}, u32[]{:S(2)}, u32[]{:S(2)}) %collective-permute-start) | collective-permute-done | bytes 64 | tf_op jit(solution)/shard_map/ppermute | solution.py:13
  76.6 0.1 iota_compare_fusion.2
  76.7 0.1 broadcast_select_fusion.2
  76.8 1.5 broadcast_select_fusion.1
  78.3 0.5 fusion.60
  78.8 7.7 %copy.102 = bf16[8,512,576]{2,1,0:T(8,128)(2,1)} copy(bf16[8,512,576]{1,2,0:T(8,128)(2,1)} %collective-permute-done.2) | data formatting | bytes 9437184 | tf_op jit(solution)/shard_map/ppermute | solution.py:13
  86.6 4.7 broadcast_select_fusion
  91.2 1.9 fusion.8
  93.1 0.6 fusion.11
  93.8 0.5 fusion.50
  94.3 1.3 add_convert_fusion
  95.6 1.6 copy.107
  97.2 8.1 %all-to-all-start = ((bf16[8,2,64,512]{3,0,1,2:T(8,128)(2,1)}), bf16[8,2,64,512]{3,0,1,2:T(8,128)(2,1)S(1)}, u32[]{:S(2)}, u32[]{:S(2)}) async-start(bf16[8,2,64,512]{3,0,1,2:T(8,128)(2,1)} %copy.107), calls=%async_computation | async-start | bytes 2097152 | tf_op jit(solution)/shard_map/all_to_all | solution.py:83
  105.3 0.0 all-reduce.4.cloned.1.call-start
  105.4 15.1 %all-to-all-done = bf16[8,2,64,512]{3,0,1,2:T(8,128)(2,1)S(1)} async-done(((bf16[8,2,64,512]{3,0,1,2:T(8,128)(2,1)}), bf16[8,2,64,512]{3,0,1,2:T(8,128)(2,1)S(1)}, u32[]{:S(2)}, u32[]{:S(2)}) %all-to-all-start) | async-done | bytes 1048608 | tf_op jit(solution)/shard_map/all_to_all | solution.py:83
  120.5 6.7 %convolution_bitcast_fusion = f32[128,2,7168]{2,0,1:T(8,128)} fusion(bf16[4,128,7168,1]{2,1,0,3:T(8,128)(2,1)} %bitcast.61, bf16[16,8,2,4,512]{4,1,2,3,0:T(8,128)(2,1)S(1)} %bitcast.62, bf16[4,512,128]{2,1,0:T(8,128)(2,1)S(1)} %copy-done), kind=kOutput, calls=%fused_computation.1 | convolution fusion | flops 2013396992 | bytes 16252928 | tf_op jit(solution)/shard_map/rshv,hvd->rsd/dot_general | solution.py:87
  127.2 1.9 add_dynamic-update-slice_fusion
  129.1 0.0 all-reduce.4.cloned.1.call-update
  129.1 0.2 all-gather.2.cloned.1.call-start
  129.3 0.4 copy-done.8
  129.8 0.1 copy.112
  129.9 0.1 reshape.167
  130.0 0.3 reduce-window.9
  130.3 0.1 slice.15
  130.4 0.1 copy.111
  130.6 0.2 eq.65
  130.7 0.1 slice_reduce_fusion
  130.9 0.1 add_bitcast_fusion
  130.9 127.7 %all-reduce.4.cloned.1.call-done = f32[128,2,7168]{2,0,1:T(8,128)} async-done(((f32[128,2,7168]{2,0,1:T(8,128)}), f32[128,2,7168]{2,0,1:T(8,128)}) %all-reduce.4.cloned.1.call-update) | async-done | bytes 7340048 | tf_op jit(solution)/shard_map/psum | solution.py:97
  258.7 3.8 multiply_reduce_fusion
  262.5 1.3 copy-done.2
  263.8 1.0 multiply_convert_fusion
  264.8 5.6 copy.113
  270.4 8.4 %reshape.169 = bf16[256,7168]{1,0:T(8,128)(2,1)} reshape(bf16[128,2,7168]{2,1,0:T(2,128)(2,1)} %copy.113) | data formatting | bytes 7340032 | tf_op jit(solution)/shard_map/reshape | solution.py:103
  278.8 3.7 convolution_convert_fusion
  282.6 0.0 all-gather.2.cloned.1.call-update
  282.6 0.3 reduce-scatter.2.cloned.1.call-start
  282.8 44.9 %all-gather.2.cloned.1.call-done = bf16[512,7168]{1,0:T(8,128)(2,1)} async-done(((bf16[64,7168]{1,0:T(8,128)(2,1)}), bf16[512,7168]{1,0:T(8,128)(2,1)}) %all-gather.2.cloned.1.call-update) | async-done | bytes 7340048 | tf_op jit(solution)/shard_map/all_gather | solution.py:124
  327.7 6.2 fusion.6
  333.9 18.2 %fusion.2 = f32[512,7168]{1,0:T(8,128)} fusion(bf16[1,256,7168]{2,1,0:T(8,128)(2,1)} %param.27, bf16[512,7168]{1,0:T(8,128)(2,1)} %all-gather.2.cloned.1.call-done, bf16[1,7168,256]{2,1,0:T(8,128)(2,1)} %param.26, f32[512,256]{1,0:T(8,128)S(1)} %fusion.6), kind=kOutput, calls=%fused_computation.8 | convolution fusion | flops 3758882816 | bytes 29884416 | tf_op jit(solution)/shard_map/dot_general | solution.py:130
  352.1 0.0 reduce-scatter.2.cloned.1.call-update
  352.1 0.1 copy.114
  352.3 0.1 eq.68
  352.4 0.3 copy-done.11
  352.8 0.6 dynamic-slice.1
  354.0 1.1 dynamic-slice_convert_fusion.1
  355.1 0.9 copy.118
  356.0 3.1 fusion.21
  359.1 0.1 mul.76
  359.3 0.1 copy.116
  359.4 0.1 div.59
  359.5 0.1 copy.115
  359.6 0.1 copy.117
  359.7 0.1 mul.77
  359.9 74.9 %reduce-scatter.2.cloned.1.call-done = f32[64,7168]{1,0:T(8,128)} async-done(((f32[512,7168]{1,0:T(8,128)}), f32[64,7168]{1,0:T(8,128)}) %reduce-scatter.2.cloned.1.call-update) | async-done | bytes 1835024 | tf_op jit(solution)/shard_map/reduce_scatter | solution.py:129
  434.8 5.6 convolution_multiply_fusion
  440.4 9.3 %reshape.170 = f32[128,2,7168]{2,1,0:T(2,128)} reshape(f32[256,7168]{1,0:T(8,128)} %convolution_multiply_fusion) | data formatting | bytes 14680064 | tf_op jit(solution)/shard_map/reshape | solution.py:140
  449.8 167.4 %all-reduce.5 = bf16[128,2,7168]{2,1,0:T(2,128)(2,1)} all-reduce(f32[128,2,7168]{2,1,0:T(2,128)} %reshape.170), channel_id=3, replica_groups=mesh['attn'=8,'ffn'=16] {'ffn'}, use_global_device_ids=true, to_apply=%region_13.14.clone | all-reduce | flops 1835008 | bytes 11010048
  617.1 1.8 dynamic-slice_convert_fusion
  (39 shorter events, 0.3 us)
Async XLA Ops:
  7.2 113.4 %copy-start = (bf16[4,512,128]{2,1,0:T(8,128)(2,1)S(1)}, bf16[4,512,128]{2,1,0:T(8,128)(2,1)}, u32[]{:S(2)}) copy-start(bf16[4,512,128]{2,1,0:T(8,128)(2,1)} %param.20) | copy-start | bytes 1572868
  7.2 69.5 %copy-start.7 = (bf16[8,2,576]{2,1,0:T(2,128)(2,1)S(1)}, bf16[8,2,576]{2,1,0:T(2,128)(2,1)}, u32[]{:S(2)}) copy-start(bf16[8,2,576]{2,1,0:T(2,128)(2,1)} %param.16) | copy-start | bytes 55300
  7.2 69.6 %copy-start.3 = (bf16[8,2,64,576]{3,2,1,0:T(8,128)(2,1)S(1)}, bf16[8,2,64,576]{3,2,1,0:T(8,128)(2,1)}, u32[]{:S(2)}) copy-start(bf16[8,2,64,576]{3,2,1,0:T(8,128)(2,1)} %param.14) | copy-start | bytes 3538948
  7.2 69.4 %copy-start.10 = (s32[8]{0:T(128)S(1)}, s32[8]{0:T(128)}, u32[]{:S(2)}) copy-start(s32[8]{0:T(128)} %param.17) | copy-start | bytes 100
  7.2 11.0 %copy-start.9 = (s32[1,8]{1,0:T(1,128)S(1)}, s32[1,8]{1,0:T(1,128)}, u32[]{:S(2)}) copy-start(s32[1,8]{1,0:T(1,128)} %param.18) | copy-start | bytes 100
  7.2 71.6 %collective-permute-start.2 = (bf16[8,512,576]{1,2,0:T(8,128)(2,1)}, bf16[8,512,576]{1,2,0:T(8,128)(2,1)}, u32[]{:S(2)}, u32[]{:S(2)}) collective-permute-start(bf16[8,512,576]{1,2,0:T(8,128)(2,1)} %param.15), channel_id=1, source_target_pairs={{0,16},{16,32},{32,48},{48,64},{64,80},{80,96},{96,112},{112,0},{1... | collective-permute-start | bytes 14155784 | tf_op jit(solution)/shard_map/ppermute | solution.py:13
  7.2 69.4 %collective-permute-start.3 = (bf16[8,2,576]{2,1,0:T(2,128)(2,1)}, bf16[8,2,576]{2,1,0:T(2,128)(2,1)S(1)}, u32[]{:S(2)}, u32[]{:S(2)}) collective-permute-start(bf16[8,2,576]{2,1,0:T(2,128)(2,1)} %param.16), channel_id=1, source_target_pairs={{0,16},{16,32},{32,48},{48,64},{64,80},{80,96},{96,112},{112,0},{1... | collective-permute-start | bytes 55304 | tf_op jit(solution)/shard_map/ppermute | solution.py:13
  8.9 67.8 %collective-permute-start.1 = (bf16[8,2,64,576]{3,2,1,0:T(8,128)(2,1)}, bf16[8,2,64,576]{3,2,1,0:T(8,128)(2,1)}, u32[]{:S(2)}, u32[]{:S(2)}) collective-permute-start(bf16[8,2,64,576]{3,2,1,0:T(8,128)(2,1)} %param.14), channel_id=1, source_target_pairs={{0,16},{16,32},{32,48},{48,64},{64,80},{80,96},{96,112},{112,0},{1... | collective-permute-start | bytes 3538952 | tf_op jit(solution)/shard_map/ppermute | solution.py:13
  9.0 67.6 %collective-permute-start = (s32[8]{0:T(128)}, s32[8]{0:T(128)S(1)}, u32[]{:S(2)}, u32[]{:S(2)}) collective-permute-start(s32[8]{0:T(128)} %param.17), channel_id=1, source_target_pairs={{0,16},{16,32},{32,48},{48,64},{64,80},{80,96},{96,112},{112,0},{1... | collective-permute-start | bytes 104 | tf_op jit(solution)/shard_map/ppermute | solution.py:13
  97.2 23.3 %all-to-all-start = ((bf16[8,2,64,512]{3,0,1,2:T(8,128)(2,1)}), bf16[8,2,64,512]{3,0,1,2:T(8,128)(2,1)S(1)}, u32[]{:S(2)}, u32[]{:S(2)}) async-start(bf16[8,2,64,512]{3,0,1,2:T(8,128)(2,1)} %copy.107), calls=%async_computation | async-start | bytes 2097152 | tf_op jit(solution)/shard_map/all_to_all | solution.py:83
  105.3 153.3 %all-reduce.4.cloned.1.call-start = ((), (), s32[]{:S(2)}) async-start(), calls=%async_computation.2 | async-start | bytes 14680064 | tf_op jit(solution)/shard_map/psum | solution.py:97
  120.5 6.7 %copy-start.4 = (bf16[8,2,7168]{2,1,0:T(2,128)(2,1)S(1)}, bf16[8,2,7168]{2,1,0:T(2,128)(2,1)}, u32[]{:S(2)}) copy-start(bf16[8,2,7168]{2,1,0:T(2,128)(2,1)} %param.19) | copy-start | bytes 688132
  129.1 0.7 copy-start.8
  129.1 133.4 %copy-start.6 = (f32[7168]{0:T(1024)S(1)}, f32[7168]{0:T(1024)}, u32[]{:S(2)}) copy-start(f32[7168]{0:T(1024)} %param.22) | copy-start | bytes 86020
  129.1 198.6 %all-gather.2.cloned.1.call-start = ((), (), s32[]{:S(2)}) async-start(), calls=%async_computation.3 | async-start | bytes 8257536 | tf_op jit(solution)/shard_map/all_gather | solution.py:124
  258.7 5.2 copy-start.2
  282.6 152.2 %reduce-scatter.2.cloned.1.call-start = ((), (), s32[]{:S(2)}) async-start(), calls=%async_computation.4 | async-start | bytes 16515072 | tf_op jit(solution)/shard_map/reduce_scatter | solution.py:129
  352.1 0.7 copy-start.11
  352.1 3.9 copy-start.5
  440.4 178.5 %copy-start.1 = (bf16[4,512,128]{2,1,0:T(8,128)(2,1)S(1)}, bf16[4,512,128]{2,1,0:T(8,128)(2,1)}, u32[]{:S(2)}) copy-start(bf16[4,512,128]{2,1,0:T(8,128)(2,1)} %param.20) | copy-start | bytes 1572868
Sparse Core Ops, SparseCore 0:
  129.2 129.4 all-reduce.3
  282.7 44.9 all-gather.1
  352.3 82.5 reduce-scatter.1
where the time goes:
time: 627 us; the launch traced here: 625 us
  waiting for transfers between devices  321 us (51%)
  blocking collectives  167 us (27%)
  local copies, waits for them, and re-layouts  48.5 us (8%)
  matrix products  47.7 us (8%)
  between operations  14.7 us (2%)
  other arithmetic  14.2 us (2%)
  starting transfers between devices  12 us (2%)
    unnamed x1, blocking collectives  167 us
    psum x1, waiting for transfers between devices, local(): state_rows = lax.psum(partial_out + placed_rows, 'ffn')  128 us
    reduce_scatter x1, waiting for transfers between devices, local(): lax.psum_scatter(jnp.dot(rows_in, down_local, preferred_element_type=jnp....  74.9 us
    ppermute x4, waiting for transfers between devices, shifted(): lax.ppermute(value, axis, [(i, (i + by) % count) for i in range(count)])  58.3 us
    all_gather x1, waiting for transfers between devices, local(): rows_in = lax.all_gather(expert_input, 'attn', axis=0, tiled=True)  44.9 us
    dot_general x1, matrix products, local(): jnp.dot(rows_in, down_local, preferred_element_type=jnp.float32)  18.2 us
    all_to_all x1, waiting for transfers between devices, local(): lax.all_to_all(latent_out, 'ffn', split_axis=2, concat_axis=0, tiled=True)  15.1 us
  transfers between devices with their start and end apart: 8, of which 5 were waited for; matrix products, arithmetic and copies ran while one was open for 3% of the time, Pallas kernels for 0%

commit v1 on v0

--- a/solution.py
+++ b/solution.py
@@ -80,7 +80,12 @@
     head_weight = output_weight.reshape(heads_local, value_up_matrix.shape[2], model_width)
     value_rows = jnp.einsum(
         "olfb,fbw->olfw",
-        lax.all_to_all(latent_out, "ffn", split_axis=2, concat_axis=0, tiled=True),
+        jnp.concatenate(
+            lax.all_to_all(
+                jnp.stack(jnp.split(latent_out, lax.axis_size("ffn"), axis=2)), "ffn", 0, 0
+            ),
+            axis=0,
+        ),
         value_up_matrix,
         preferred_element_type=jnp.float32,
     ).astype(jnp.bfloat16)

time: 627 us -> 636 us (1.014)
  local copies, waits for them, and re-layouts: 48.5 us -> 57.3 us
    unnamed x28 -> x43, local copies, waits for them, and re-layouts: 11.5 us -> 21.2 us
where the time goes in v1:
time: 636 us; the launch traced here: 635 us
  waiting for transfers between devices  321 us (50%)
  blocking collectives  167 us (26%)
  local copies, waits for them, and re-layouts  57.3 us (9%)
  matrix products  48.4 us (8%)
  between operations  14.7 us (2%)
  other arithmetic  14.2 us (2%)
  starting transfers between devices  12 us (2%)
    unnamed x1, blocking collectives  167 us
    psum x1, waiting for transfers between devices, local(): state_rows = lax.psum(partial_out + placed_rows, 'ffn')  128 us
    reduce_scatter x1, waiting for transfers between devices, local(): lax.psum_scatter(jnp.dot(rows_in, down_local, preferred_element_type=jnp....  74.9 us
    ppermute x4, waiting for transfers between devices, shifted(): lax.ppermute(value, axis, [(i, (i + by) % count) for i in range(count)])  58.3 us
    all_gather x1, waiting for transfers between devices, local(): rows_in = lax.all_gather(expert_input, 'attn', axis=0, tiled=True)  44.9 us
    unnamed x43, local copies, waits for them, and re-layouts  21.2 us
    dot_general x1, matrix products, local(): jnp.dot(rows_in, down_local, preferred_element_type=jnp.float32)  18.2 us
    all_to_all x1, waiting for transfers between devices, local(): lax.all_to_all(jnp.stack(jnp.split(latent_out, lax.axis_size('ffn'), axis...  15.1 us
  transfers between devices with their start and end apart: 8, of which 5 were waited for; matrix products, arithmetic and copies ran while one was open for 3% of the time, Pallas kernels for 0%

profile of v1, /device:TPU:0, one launch (start us, length us, event | category | flops | bytes accessed | tf_op | source)
XLA Modules:
  0.0 634.9 jit_solution(3954611770264681464)
XLA Ops:
  7.2 1.7 collective-permute-start.3
  9.0 1.6 collective-permute-start
  10.5 7.7 %copy.82 = bf16[8,512,576]{2,1,0:T(8,128)(2,1)} copy(bf16[8,512,576]{1,2,0:T(8,128)(2,1)} %param.15) | data formatting | bytes 9437184 | tf_op args[1]
  18.3 58.3 %collective-permute-done = s32[8]{0:T(128)S(1)} collective-permute-done((s32[8]{0:T(128)}, s32[8]{0:T(128)S(1)}, u32[]{:S(2)}, u32[]{:S(2)}) %collective-permute-start) | collective-permute-done | bytes 64 | tf_op jit(solution)/shard_map/ppermute | solution.py:13
  76.8 1.5 broadcast_select_fusion.1
  78.3 0.5 fusion.76
  78.8 7.7 %copy.81 = bf16[8,512,576]{2,1,0:T(8,128)(2,1)} copy(bf16[8,512,576]{1,2,0:T(8,128)(2,1)} %collective-permute-done.2) | data formatting | bytes 9437184 | tf_op jit(solution)/shard_map/ppermute | solution.py:13
  86.6 4.7 broadcast_select_fusion
  91.2 1.9 fusion.8
  93.1 0.6 fusion.11
  93.8 0.5 fusion.66
  94.3 1.3 add_convert_fusion
  95.6 0.6 fusion.58
  96.3 0.7 fusion.57
  96.9 0.6 fusion.56
  97.6 0.7 fusion.55
  98.2 0.6 fusion.54
  98.8 0.7 fusion.53
  99.5 0.6 fusion.52
  100.1 0.7 fusion.51
  100.8 0.6 fusion.50
  101.4 0.7 fusion.49
  102.1 0.6 fusion.48
  102.7 0.7 fusion.47
  103.4 0.6 fusion.46
  104.0 0.7 fusion.45
  104.7 0.6 fusion.44
  105.3 0.7 fusion.43
  106.0 8.1 %all-to-all-start = ((bf16[16,8,2,4,512]{4,3,2,1,0:T(4,128)(2,1)}), bf16[16,8,2,4,512]{4,3,2,1,0:T(4,128)(2,1)S(1)}, u32[]{:S(2)}, u32[]{:S(2)}) async-start(bf16[16,8,2,4,512]{4,3,2,1,0:T(4,128)(2,1)} %fusion.43), calls=%async_computation | async-start | bytes 2097152 | tf_op jit(solution)/shard_map/all_to_all | solution.py:84
  114.2 15.1 %all-to-all-done = bf16[16,8,2,4,512]{4,3,2,1,0:T(4,128)(2,1)S(1)} async-done(((bf16[16,8,2,4,512]{4,3,2,1,0:T(4,128)(2,1)}), bf16[16,8,2,4,512]{4,3,2,1,0:T(4,128)(2,1)S(1)}, u32[]{:S(2)}, u32[]{:S(2)}) %all-to-all-start) | async-done | bytes 1048608 | tf_op jit(solution)/shard_map/all_to_all | solution.py:84
  129.3 7.3 %convolution_bitcast_fusion = f32[128,2,7168]{2,0,1:T(8,128)} fusion(bf16[4,128,7168,1]{2,1,0,3:T(8,128)(2,1)} %bitcast.122, bf16[16,8,2,4,512]{4,3,2,1,0:T(4,128)(2,1)S(1)} %all-to-all-done, bf16[4,512,128]{2,1,0:T(8,128)(2,1)S(1)} %copy-done), kind=kOutput, calls=%fused_computation.1 | convolution fusion | flops 2013396992 | bytes 16252928 | tf_op jit(solution)/shard_map/rshv,hvd->rsd/dot_general | solution.py:92
  136.7 1.9 add_dynamic-update-slice_fusion
  138.6 0.2 all-gather.2.cloned.1.call-start
  138.8 0.4 copy-done.8
  139.3 0.1 reshape.171
  139.5 0.3 reduce-window.9
  139.9 0.1 copy.88
  140.1 0.2 eq.65
  140.4 127.7 %all-reduce.4.cloned.1.call-done = f32[128,2,7168]{2,0,1:T(8,128)} async-done(((f32[128,2,7168]{2,0,1:T(8,128)}), f32[128,2,7168]{2,0,1:T(8,128)}) %all-reduce.4.cloned.1.call-update) | async-done | bytes 7340048 | tf_op jit(solution)/shard_map/psum | solution.py:102
  268.1 3.8 multiply_reduce_fusion
  272.0 1.3 copy-done.2
  273.3 1.0 multiply_convert_fusion
  274.3 5.6 copy.90
  279.9 8.4 %reshape.173 = bf16[256,7168]{1,0:T(8,128)(2,1)} reshape(bf16[128,2,7168]{2,1,0:T(2,128)(2,1)} %copy.90) | data formatting | bytes 7340032 | tf_op jit(solution)/shard_map/reshape | solution.py:108
  288.3 3.7 convolution_convert_fusion
  292.0 0.3 reduce-scatter.2.cloned.1.call-start
  292.3 44.9 %all-gather.2.cloned.1.call-done = bf16[512,7168]{1,0:T(8,128)(2,1)} async-done(((bf16[64,7168]{1,0:T(8,128)(2,1)}), bf16[512,7168]{1,0:T(8,128)(2,1)}) %all-gather.2.cloned.1.call-update) | async-done | bytes 7340048 | tf_op jit(solution)/shard_map/all_gather | solution.py:129
  337.2 6.2 fusion.6
  343.4 18.2 %fusion.2 = f32[512,7168]{1,0:T(8,128)} fusion(bf16[1,256,7168]{2,1,0:T(8,128)(2,1)} %param.27, bf16[512,7168]{1,0:T(8,128)(2,1)} %all-gather.2.cloned.1.call-done, bf16[1,7168,256]{2,1,0:T(8,128)(2,1)} %param.26, f32[512,256]{1,0:T(8,128)S(1)} %fusion.6), kind=kOutput, calls=%fused_computation.8 | convolution fusion | flops 3758882816 | bytes 29884416 | tf_op jit(solution)/shard_map/dot_general | solution.py:135
  361.6 0.1 copy.91
  361.8 0.1 eq.68
  361.9 0.3 copy-done.11
  362.2 0.6 dynamic-slice.1
  363.5 1.1 dynamic-slice_convert_fusion.1
  364.5 0.9 copy.95
  365.5 3.1 fusion.21
  368.6 0.1 mul.76
  368.8 0.1 div.59
  369.2 0.1 mul.77
  369.3 74.9 %reduce-scatter.2.cloned.1.call-done = f32[64,7168]{1,0:T(8,128)} async-done(((f32[512,7168]{1,0:T(8,128)}), f32[64,7168]{1,0:T(8,128)}) %reduce-scatter.2.cloned.1.call-update) | async-done | bytes 1835024 | tf_op jit(solution)/shard_map/reduce_scatter | solution.py:134
  444.3 5.6 convolution_multiply_fusion
  449.9 9.3 %reshape.174 = f32[128,2,7168]{2,1,0:T(2,128)} reshape(f32[256,7168]{1,0:T(8,128)} %convolution_multiply_fusion) | data formatting | bytes 14680064 | tf_op jit(solution)/shard_map/reshape | solution.py:145
  459.2 167.4 %all-reduce.5 = bf16[128,2,7168]{2,1,0:T(2,128)(2,1)} all-reduce(f32[128,2,7168]{2,1,0:T(2,128)} %reshape.174), channel_id=3, replica_groups=mesh['attn'=8,'ffn'=16] {'ffn'}, use_global_device_ids=true, to_apply=%region_13.14.clone | all-reduce | flops 1835008 | bytes 11010048
  626.6 1.8 dynamic-slice_convert_fusion
  (54 shorter events, 1.2 us)
Async XLA Ops:
  7.2 122.2 %copy-start = (bf16[4,512,128]{2,1,0:T(8,128)(2,1)S(1)}, bf16[4,512,128]{2,1,0:T(8,128)(2,1)}, u32[]{:S(2)}) copy-start(bf16[4,512,128]{2,1,0:T(8,128)(2,1)} %param.20) | copy-start | bytes 1572868
  7.2 69.5 %copy-start.7 = (bf16[8,2,576]{2,1,0:T(2,128)(2,1)S(1)}, bf16[8,2,576]{2,1,0:T(2,128)(2,1)}, u32[]{:S(2)}) copy-start(bf16[8,2,576]{2,1,0:T(2,128)(2,1)} %param.16) | copy-start | bytes 55300
  7.2 69.6 %copy-start.3 = (bf16[8,2,64,576]{3,2,1,0:T(8,128)(2,1)S(1)}, bf16[8,2,64,576]{3,2,1,0:T(8,128)(2,1)}, u32[]{:S(2)}) copy-start(bf16[8,2,64,576]{3,2,1,0:T(8,128)(2,1)} %param.14) | copy-start | bytes 3538948
  7.2 69.4 %copy-start.10 = (s32[8]{0:T(128)S(1)}, s32[8]{0:T(128)}, u32[]{:S(2)}) copy-start(s32[8]{0:T(128)} %param.17) | copy-start | bytes 100
  7.2 11.0 %copy-start.9 = (s32[1,8]{1,0:T(1,128)S(1)}, s32[1,8]{1,0:T(1,128)}, u32[]{:S(2)}) copy-start(s32[1,8]{1,0:T(1,128)} %param.18) | copy-start | bytes 100
  7.2 71.6 %collective-permute-start.2 = (bf16[8,512,576]{1,2,0:T(8,128)(2,1)}, bf16[8,512,576]{1,2,0:T(8,128)(2,1)}, u32[]{:S(2)}, u32[]{:S(2)}) collective-permute-start(bf16[8,512,576]{1,2,0:T(8,128)(2,1)} %param.15), channel_id=1, source_target_pairs={{0,16},{16,32},{32,48},{48,64},{64,80},{80,96},{96,112},{112,0},{1... | collective-permute-start | bytes 14155784 | tf_op jit(solution)/shard_map/ppermute | solution.py:13
  7.2 69.4 %collective-permute-start.3 = (bf16[8,2,576]{2,1,0:T(2,128)(2,1)}, bf16[8,2,576]{2,1,0:T(2,128)(2,1)S(1)}, u32[]{:S(2)}, u32[]{:S(2)}) collective-permute-start(bf16[8,2,576]{2,1,0:T(2,128)(2,1)} %param.16), channel_id=1, source_target_pairs={{0,16},{16,32},{32,48},{48,64},{64,80},{80,96},{96,112},{112,0},{1... | collective-permute-start | bytes 55304 | tf_op jit(solution)/shard_map/ppermute | solution.py:13
  8.9 67.8 %collective-permute-start.1 = (bf16[8,2,64,576]{3,2,1,0:T(8,128)(2,1)}, bf16[8,2,64,576]{3,2,1,0:T(8,128)(2,1)}, u32[]{:S(2)}, u32[]{:S(2)}) collective-permute-start(bf16[8,2,64,576]{3,2,1,0:T(8,128)(2,1)} %param.14), channel_id=1, source_target_pairs={{0,16},{16,32},{32,48},{48,64},{64,80},{80,96},{96,112},{112,0},{1... | collective-permute-start | bytes 3538952 | tf_op jit(solution)/shard_map/ppermute | solution.py:13
  9.0 67.6 %collective-permute-start = (s32[8]{0:T(128)}, s32[8]{0:T(128)S(1)}, u32[]{:S(2)}, u32[]{:S(2)}) collective-permute-start(s32[8]{0:T(128)} %param.17), channel_id=1, source_target_pairs={{0,16},{16,32},{32,48},{48,64},{64,80},{80,96},{96,112},{112,0},{1... | collective-permute-start | bytes 104 | tf_op jit(solution)/shard_map/ppermute | solution.py:13
  106.0 23.3 %all-to-all-start = ((bf16[16,8,2,4,512]{4,3,2,1,0:T(4,128)(2,1)}), bf16[16,8,2,4,512]{4,3,2,1,0:T(4,128)(2,1)S(1)}, u32[]{:S(2)}, u32[]{:S(2)}) async-start(bf16[16,8,2,4,512]{4,3,2,1,0:T(4,128)(2,1)} %fusion.43), calls=%async_computation | async-start | bytes 2097152 | tf_op jit(solution)/shard_map/all_to_all | solution.py:84
  114.1 154.0 %all-reduce.4.cloned.1.call-start = ((), (), s32[]{:S(2)}) async-start(), calls=%async_computation.2 | async-start | bytes 14680064 | tf_op jit(solution)/shard_map/psum | solution.py:102
  129.3 7.3 %copy-start.4 = (bf16[8,2,7168]{2,1,0:T(2,128)(2,1)S(1)}, bf16[8,2,7168]{2,1,0:T(2,128)(2,1)}, u32[]{:S(2)}) copy-start(bf16[8,2,7168]{2,1,0:T(2,128)(2,1)} %param.19) | copy-start | bytes 688132
  138.5 0.7 copy-start.8
  138.5 133.4 %copy-start.6 = (f32[7168]{0:T(1024)S(1)}, f32[7168]{0:T(1024)}, u32[]{:S(2)}) copy-start(f32[7168]{0:T(1024)} %param.22) | copy-start | bytes 86020
  138.6 198.6 %all-gather.2.cloned.1.call-start = ((), (), s32[]{:S(2)}) async-start(), calls=%async_computation.3 | async-start | bytes 8257536 | tf_op jit(solution)/shard_map/all_gather | solution.py:129
  268.1 5.2 copy-start.2
  292.0 152.2 %reduce-scatter.2.cloned.1.call-start = ((), (), s32[]{:S(2)}) async-start(), calls=%async_computation.4 | async-start | bytes 16515072 | tf_op jit(solution)/shard_map/reduce_scatter | solution.py:134
  361.6 0.7 copy-start.11
  361.6 3.9 copy-start.5
  449.9 178.5 %copy-start.1 = (bf16[4,512,128]{2,1,0:T(8,128)(2,1)S(1)}, bf16[4,512,128]{2,1,0:T(8,128)(2,1)}, u32[]{:S(2)}) copy-start(bf16[4,512,128]{2,1,0:T(8,128)(2,1)} %param.20) | copy-start | bytes 1572868
Sparse Core Ops, SparseCore 0:
  138.7 129.4 all-reduce.3
  292.2 44.9 all-gather.1
  361.7 82.5 reduce-scatter.1
